TPU v7x, 32 devices: a whole 2x2x4 slice. The times are simulated.
32 devices in a mesh: batch: 2 (over x), rows: 16 (over z, y, core).
Axes of the slice: x: 2, y: 2, z: 4, core: 2. Of those that a mesh axis runs over, the one named last changes fastest.
Arguments:
- layer_input: bfloat16 [2, 64, 64, 2048], P('batch', 'rows'), may hold values from -6 to 6
- pre_activation: bfloat16 [2, 64, 64, 2048], P('batch', 'rows'), may hold values from -6 to 6
- cotangent: bfloat16 [2, 64, 64, 2048], P('batch', 'rows'), may hold values from -6 to 6
- weight: bfloat16 [64, 64], replicated, may hold values from -0.75 to 0.75
- spectral: bfloat16 [2304, 64, 128], P('rows'), may hold values from -6 to 6
- slab_ids: int32 [2, 32], P('batch'), may hold values from 0 to 2047, as said below
- extents: int32 [2, 32], P('batch'), may hold values from 1 to 2048, as said below
Outputs:
- grad_input: bfloat16 [2, 64, 64, 2048], P('batch', 'rows')
- grad_spectral: float32 [2304, 64, 128], P('rows')
- grad_weight: float32 [64, 64], replicated
Inputs may be any that keep to these rules, and one draw needn't show every extreme that they name: `slab_ids`: within a sample the 32 slab numbers are distinct and include 0 and 2047; slots 2 k to 2 k + 1 are stored on index k of rows. `extents`: A slot's extent counts its slab's live columns from column 0.
All inputs are finite; a program needn't handle non-finite values.
Results may differ from a plain program's by a relative error of at most 0.0085.
Values may be sent and summed in bfloat16 or wider, within the bound.
No kernel may reach another device: no remote copies, remote signals or barrier semaphores. Data moves between devices by JAX's collectives and lax.ppermute only.
A program may use at most 128 MiB of HBM per device.

v0:
```python
import math
import jax
import jax.numpy as jnp
from jax import lax
from jax.sharding import PartitionSpec as P

PA = 48
SLAB = 2
NR = 4096
MODES = 96


def column_table(column_count, freq_count):
    column_index = jnp.arange(column_count, dtype=jnp.int32)
    freq_index = jnp.arange(freq_count, dtype=jnp.int32)
    phase = column_index[:, None] * freq_index[None, :] % column_count
    angle = phase.astype(jnp.float32) * (2.0 * math.pi / column_count)
    return jnp.concatenate([jnp.cos(angle), -jnp.sin(angle)], axis=1).astype(jnp.bfloat16)


def row_table(positions, row_total, freq_count):
    freq_index = jnp.arange(freq_count, dtype=jnp.int32) - freq_count // 2
    phase = jnp.mod(freq_index[:, None] * positions[None, :], row_total)
    angle = phase.astype(jnp.float32) * (2.0 * math.pi / row_total)
    return jnp.concatenate([jnp.cos(angle), jnp.sin(angle)], axis=0).astype(jnp.bfloat16)


def stored_positions(slab_list, slab_rows):
    offsets = jnp.tile(jnp.arange(slab_rows, dtype=jnp.int32), slab_list.shape[0])
    return jnp.repeat(slab_list, slab_rows) * slab_rows + offsets


def gelu_slope(values):
    return (
        0.5 * (1.0 + lax.erf(values * 0.7071067811865476))
        + values * jnp.exp(-0.5 * values * values) * 0.3989422804014327
    )


def row_combine(row_sums, scale):
    upper = row_sums[0]
    lower = row_sums[1]
    real_part = upper[:, :, 0] + lower[:, :, 1]
    imag_part = upper[:, :, 1] - lower[:, :, 0]
    return (jnp.stack([real_part, imag_part], axis=2) * scale).astype(jnp.bfloat16)


def to_blocks(spectra, half_modes):
    chans = spectra.shape[1]
    shaped = spectra.reshape(half_modes, 2, chans, 2, half_modes, 2)
    return shaped.transpose(2, 3, 1, 5, 0, 4).reshape(chans, 2, 2, 2, half_modes * half_modes)


def from_blocks(blocked, half_modes):
    chans = blocked.shape[0]
    shaped = blocked.reshape(chans, 2, 2, 2, half_modes, half_modes)
    return shaped.transpose(4, 2, 0, 1, 5, 3).reshape(2 * half_modes, chans, 2, 2 * half_modes)


def factor_pair(owned, chans):
    input_modes = owned[:chans]
    grad_out = owned[chans:]
    factor_left = input_modes.transpose(4, 0, 1, 2, 3).reshape(owned.shape[4], chans, 8)
    real_out = grad_out[:, 0]
    imag_out = grad_out[:, 1]
    first_half = jnp.stack([real_out, imag_out], axis=1)
    second_half = jnp.stack([imag_out, -real_out], axis=1)
    stacked = jnp.concatenate([first_half, second_half], axis=0)
    factor_right = stacked.transpose(4, 0, 1, 2, 3).reshape(owned.shape[4], 2 * chans, 8)
    return (factor_left, factor_right)


def modes_to_channels(grad_modes):
    blocks = grad_modes.shape[0]
    chans = grad_modes.shape[1]
    return grad_modes.reshape(blocks, chans, 2, 2, 2).transpose(1, 2, 3, 4, 0)


def row_adjoint(rowtab, grad_grid, scale):
    real_part = grad_grid[:, :, 0]
    imag_part = grad_grid[:, :, 1]
    upper = jnp.stack([real_part, imag_part], axis=2)
    lower = jnp.stack([-imag_part, real_part], axis=2)
    joined = jnp.concatenate([upper, lower], axis=0)
    summed = jnp.dot(
        rowtab.T, joined.reshape(joined.shape[0], -1), preferred_element_type=jnp.float32
    )
    return (summed * scale).astype(jnp.bfloat16)


def shards(layer_input, pre_activation, cotangent, weight, spectral, slab_ids, extents):
    batch_devices = lax.axis_size("batch")
    local_rows = layer_input.shape[1]
    channels = layer_input.shape[2]
    column_count = layer_input.shape[3]
    slab_list = slab_ids[0]
    active = slab_list.shape[0]
    slots = local_rows // SLAB
    scale = 1.0 / math.sqrt(NR * column_count)
    position = lax.axis_index("rows")
    own_extents = lax.dynamic_slice_in_dim(extents[0], position * slots, slots)
    column_index = jnp.arange(column_count, dtype=jnp.int32)
    alive = column_index[None, :] < jnp.repeat(own_extents, SLAB)[:, None]
    mask_half = alive.astype(jnp.bfloat16)
    mask_full = alive.astype(jnp.float32)
    masked_in = layer_input[0] * mask_half[:, None, :]
    grad_pre = (
        cotangent[0].astype(jnp.float32)
        * mask_full[:, None, :]
        * gelu_slope(pre_activation[0].astype(jnp.float32))
    ).astype(jnp.bfloat16)
    coltab = column_table(column_count, MODES)
    stacked = jnp.concatenate([masked_in, grad_pre], axis=1)
    colspec = jnp.dot(stacked.reshape(-1, column_count), coltab, preferred_element_type=jnp.float32)
    colspec = colspec.reshape(local_rows, 2 * channels, 2 * MODES).astype(jnp.bfloat16)
    gathered_rows = lax.all_to_all(colspec, "rows", split_axis=1, concat_axis=0, tiled=True)
    all_rows = gathered_rows.shape[0]
    owned_channels = gathered_rows.shape[1]
    rowtab = row_table(stored_positions(slab_list, SLAB), NR, MODES)
    row_sums = jnp.dot(
        rowtab, gathered_rows.reshape(all_rows, -1), preferred_element_type=jnp.float32
    )
    spectra = row_combine(row_sums.reshape(2, MODES, owned_channels, 2, MODES), scale)
    owned = lax.all_to_all(to_blocks(spectra, PA), "rows", split_axis=4, concat_axis=0, tiled=True)
    factor_left, factor_right = factor_pair(owned, channels)
    grad_modes = jnp.einsum(
        "bix,bxk->bik", spectral, factor_right, preferred_element_type=jnp.float32
    ).astype(jnp.bfloat16)
    own_grad = jnp.einsum(
        "bik,bxk->bix", factor_left, factor_right, preferred_element_type=jnp.float32
    )
    grad_spectral = lax.psum(own_grad, "batch")
    returned = lax.all_to_all(
        modes_to_channels(grad_modes), "rows", split_axis=0, concat_axis=4, tiled=True
    )
    rowback = row_adjoint(rowtab, from_blocks(returned, PA), scale)
    rowback = rowback.reshape(all_rows, -1, 2 * MODES)
    local_back = lax.all_to_all(rowback, "rows", split_axis=0, concat_axis=1, tiled=True)
    spatial = jnp.dot(
        local_back.reshape(-1, 2 * MODES), coltab.T, preferred_element_type=jnp.float32
    )
    spatial = spatial.reshape(local_rows, channels, column_count)
    row_weight = jnp.broadcast_to(weight, (local_rows, channels, channels))
    direct = jnp.einsum("rio,roc->ric", row_weight, grad_pre, preferred_element_type=jnp.float32)
    grad_input = ((spatial + direct) * mask_full[:, None, :]).astype(jnp.bfloat16)[None]
    row_partial = jnp.einsum(
        "ric,roc->rio", masked_in, grad_pre, preferred_element_type=jnp.float32
    )
    local_weight = jnp.sum(row_partial, axis=0)
    grad_weight = lax.psum(local_weight, ("batch", "rows"))
    grad_weight = grad_weight * (1.0 / math.sqrt(batch_devices * active * SLAB * column_count))
    return (grad_input, grad_spectral, grad_weight)


def solution(mesh):
    return jax.shard_map(
        shards,
        mesh=mesh,
        in_specs=(
            P("batch", "rows", None, None),
            P("batch", "rows", None, None),
            P("batch", "rows", None, None),
            P(),
            P("rows", None, None),
            P("batch", None),
            P("batch", None),
        ),
        out_specs=(P("batch", "rows", None, None), P("rows", None, None), P()),
        check_vma=False,
    )
```

profile of v0, /device:TPU:0, one launch (start us, length us, event | category | flops | bytes accessed | tf_op | source)
XLA Modules:
  0.0 304.3 jit_solution(13098841507869636662)
XLA Ops:
  7.2 3.9 %negate_convert_fusion = (bf16[2048,96]{0,1:T(8,128)(2,1)}, bf16[2048,96]{0,1:T(8,128)(2,1)}) fusion(), kind=kLoop, calls=%fused_computation.40 | loop fusion | flops 3342336 | bytes 786432 | tf_op jit(solution)/shard_map/convert.3
  11.1 0.7 dynamic-slice_bitcast_fusion
  12.0 1.4 bitcast_multiply_fusion
  13.5 0.3 copy-done.5
  13.8 1.1 fusion.15
  15.1 1.6 fusion.17
  16.6 1.8 copy.52
  18.4 7.5 %all-to-all-start = ((bf16[4,128,192]{2,0,1:T(4,128)(2,1)}), bf16[4,128,192]{2,0,1:T(4,128)(2,1)}, u32[]{:S(2)}, u32[]{:S(2)}) async-start(bf16[4,128,192]{2,0,1:T(4,128)(2,1)} %copy.52), calls=%async_computation | async-start | bytes 524288 | tf_op jit(solution)/shard_map/all_to_all | solution.py:116
  25.9 0.2 all-reduce.2.cloned.1.call-start
  26.3 0.3 cosine_convert_fusion.1
  26.6 9.3 %all-to-all-done = bf16[4,128,192]{2,0,1:T(4,128)(2,1)} async-done(((bf16[4,128,192]{2,0,1:T(4,128)(2,1)}), bf16[4,128,192]{2,0,1:T(4,128)(2,1)}, u32[]{:S(2)}, u32[]{:S(2)}) %all-to-all-start) | async-done | bytes 196640 | tf_op jit(solution)/shard_map/all_to_all | solution.py:116
  35.9 1.0 copy.87
  36.9 0.7 copy.54
  37.7 1.9 reshape.119
  39.5 1.2 fusion.38
  40.7 1.1 fusion.43
  41.9 3.0 squeeze.7
  44.8 3.1 %fusion.45 = (f32[96,8,1,96]{3,2,1,0:T(1,128)}, f32[96,8,1,96]{3,2,1,0:T(1,128)}) fusion(f32[96,8,2,96]{3,2,1,0:T(2,128)} %squeeze.7), kind=kLoop, calls=%fused_computation.82 | loop fusion | bytes 1179648 | tf_op jit(solution)/shard_map/slice | solution.py:43
  47.9 4.2 %copy.79 = f32[96,8,1,96]{1,3,0,2:T(8,128)} copy(f32[96,8,1,96]{3,2,1,0:T(1,128)} %get-tuple-element.10) | data formatting | bytes 589824
  52.1 3.0 squeeze.8
  55.1 2.9 fusion.44
  58.0 4.2 %copy.80 = f32[96,8,1,96]{1,3,0,2:T(8,128)} copy(f32[96,8,1,96]{3,2,1,0:T(1,128)} %get-tuple-element.8) | data formatting | bytes 589824
  62.2 6.9 %sub.9 = f32[96,8,1,96]{1,3,0,2:T(8,128)} subtract(f32[96,8,1,96]{1,3,0,2:T(8,128)} %copy.79, f32[96,8,1,96]{1,3,0,2:T(8,128)} %copy.80) | non-fusion elementwise | flops 73728 | bytes 884736 | tf_op jit(solution)/shard_map/sub | solution.py:44
  69.1 6.2 %copy.60 = f32[48,2,8,1,48,2]{4,2,5,3,1,0:T(8,128)} copy(f32[48,2,8,1,48,2]{2,5,4,1,0,3:T(2,128)} %bitcast.84) | data formatting | bytes 589824 | tf_op jit(solution)/shard_map/stack | solution.py:45
  75.3 4.2 %copy.77 = f32[96,8,1,96]{1,3,0,2:T(8,128)} copy(f32[96,8,1,96]{3,2,1,0:T(1,128)} %get-tuple-element.9) | data formatting | bytes 589824
  79.5 4.2 %copy.78 = f32[96,8,1,96]{1,3,0,2:T(8,128)} copy(f32[96,8,1,96]{3,2,1,0:T(1,128)} %get-tuple-element.7) | data formatting | bytes 589824
  83.7 6.9 %add.60 = f32[96,8,1,96]{1,3,0,2:T(8,128)} add(f32[96,8,1,96]{1,3,0,2:T(8,128)} %copy.77, f32[96,8,1,96]{1,3,0,2:T(8,128)} %copy.78) | non-fusion elementwise | flops 73728 | bytes 884736 | tf_op jit(solution)/shard_map/add | solution.py:43
  90.6 6.2 %copy.59 = f32[48,2,8,1,48,2]{4,2,5,3,1,0:T(8,128)} copy(f32[48,2,8,1,48,2]{2,5,4,1,0,3:T(2,128)} %bitcast.85) | data formatting | bytes 589824 | tf_op jit(solution)/shard_map/stack | solution.py:45
  96.8 2.5 fusion.24
  99.3 9.3 %copy.74 = bf16[8,2,2,2,48,48]{0,3,2,1,5,4:T(2,128)(2,1)} copy(bf16[8,2,2,2,48,48]{5,0,3,1,2,4:T(8,128)(2,1)} %fusion.24) | data formatting | bytes 589824 | tf_op jit(solution)/shard_map/reshape | solution.py:51
  108.6 7.0 %reshape.131 = bf16[16,2,4608]{2,1,0:T(2,128)(2,1)} reshape(bf16[2304,2,2,2,8]{4,3,2,1,0:T(2,128)(2,1)} %bitcast.87) | data formatting | bytes 589824
  115.6 14.7 %all_to_all.60 = bf16[16,2,4608]{2,1,0:T(2,128)(2,1)} all-to-all(bf16[16,2,4608]{2,1,0:T(2,128)(2,1)} %reshape.131), channel_id=1, replica_groups=mesh['batch'=2,'rows'=16] {'rows'}, dimensions={0} | all-to-all | bytes 589824 | tf_op jit(solution)/shard_map/all_to_all | solution.py:124
  130.3 7.4 %reshape.132 = bf16[2304,2,2,2,8]{4,3,2,1,0:T(2,128)(2,1)} reshape(bf16[16,2,4608]{2,1,0:T(2,128)(2,1)} %all_to_all.60) | data formatting | bytes 589824
  137.7 12.1 %copy.75 = bf16[8,2,2,2,16,144]{5,4,0,3,2,1:T(8,128)(2,1)} copy(bf16[8,2,2,2,16,144]{0,3,2,1,5,4:T(2,128)(2,1)} %bitcast.88) | data formatting | bytes 589824 | tf_op jit(solution)/shard_map/all_to_all | solution.py:124
  149.8 1.8 fusion.46
  151.6 0.9 maximum_bitcast_fusion.1
  152.5 1.9 copy.65
  154.5 1.7 copy.85
  156.2 1.9 copy.73
  158.1 4.0 %fusion.48 = f32[144,64,128]{2,1,0:T(8,128)} fusion(bf16[144,64,8]{1,2,0:T(8,128)(2,1)} %bitcast.97, bf16[144,128,8]{1,2,0:T(8,128)(2,1)} %bitcast.91), kind=kOutput, calls=%fused_computation.85 | convolution fusion | flops 18874368 | bytes 5160960 | tf_op jit(solution)/shard_map/bik,bxk->bix/dot_general | solution.py:129
  162.1 3.0 convolution_convert_fusion
  165.1 2.0 copy.66
  167.1 4.2 %all-to-all-start.2 = ((bf16[64,2,2,2,144]{4,3,2,1,0:T(2,128)(2,1)}), bf16[64,2,2,2,144]{4,3,2,1,0:T(2,128)(2,1)}, u32[]{:S(2)}, u32[]{:S(2)}) async-start(bf16[64,2,2,2,144]{4,3,2,1,0:T(2,128)(2,1)} %bitcast.98), calls=%async_computation.2 | async-start | bytes 524288 | tf_op jit(solution)/shard_map/all_to_all | solution.py:133
  171.3 1.6 convolution_bitcast_fusion.1
  173.0 42.4 %psum.15 = f32[64,64]{1,0:T(8,128)} all-reduce(f32[64,64]{1,0:T(8,128)S(1)} %convolution_bitcast_fusion.1), channel_id=1, replica_groups=mesh['batch'=2,'rows'=16] {'batch','rows'}, use_global_device_ids=true, to_apply=%region_1.2 | all-reduce | flops 4096 | bytes 32768 | tf_op jit(solution)/shard_map/psum | solution.py:150
  215.4 1.8 copy.67
  217.2 2.1 reshape.123
  219.3 13.9 %copy.69 = bf16[48,2,4,2,48,2]{2,5,4,3,1,0:T(2,128)(2,1)} copy(bf16[48,2,4,2,48,2]{4,0,5,1,3,2:T(8,128)(2,1)} %bitcast.89) | data formatting | bytes 294912 | tf_op jit(solution)/shard_map/transpose | solution.py:57
  233.2 8.4 %copy.68 = bf16[48,2,4,2,48,2]{5,4,3,2,1,0:T(8,128)(2,1)} copy(bf16[48,2,4,2,48,2]{4,0,5,1,3,2:T(8,128)(2,1)} %bitcast.90) | data formatting | bytes 294912 | tf_op jit(solution)/shard_map/transpose | solution.py:57
  241.7 2.9 slice_negate_fusion
  244.5 3.1 %pad_maximum_fusion = bf16[96,4,2,96]{1,3,2,0:T(8,128)(2,1)} fusion(bf16[96,4,1,96]{1,3,2,0:T(8,128)(2,1)S(1)} %get-tuple-element.4, bf16[96,4,1,96]{1,3,2,0:T(8,128)(2,1)S(1)} %get-tuple-element.3), kind=kLoop, calls=%fused_computation | loop fusion | flops 73728 | bytes 294912 | tf_op jit(solution)/shard_map/stack | solution.py:83
  247.6 4.9 %copy.70 = bf16[96,4,2,96]{3,2,1,0:T(2,128)(2,1)} copy(bf16[96,4,2,96]{1,3,2,0:T(8,128)(2,1)} %pad_maximum_fusion) | data formatting | bytes 294912 | tf_op jit(solution)/shard_map/stack | solution.py:83
  252.5 1.1 concatenate.28
  253.7 17.1 %concatenate.27 = bf16[96,768]{1,0:T(8,128)(2,1)} reshape(bf16[48,2,4,2,48,2]{5,4,3,2,1,0:T(8,128)(2,1)} %copy.68) | data formatting | bytes 294912 | tf_op jit(solution)/shard_map/concatenate | solution.py:84
  270.7 1.8 fusion.20
  272.5 1.7 reshape.125
  274.2 5.3 %all-to-all-start.3 = ((bf16[64,4,192]{2,1,0:T(4,128)(2,1)}), bf16[64,4,192]{2,1,0:T(4,128)(2,1)S(1)}, u32[]{:S(2)}, u32[]{:S(2)}) async-start(bf16[64,4,192]{2,1,0:T(4,128)(2,1)} %reshape.125), calls=%async_computation.3 | async-start | bytes 262144 | tf_op jit(solution)/shard_map/all_to_all | solution.py:138
  279.6 1.4 broadcast_multiply_fusion
  281.0 6.5 %all-to-all-done.3 = bf16[64,4,192]{2,1,0:T(4,128)(2,1)S(1)} async-done(((bf16[64,4,192]{2,1,0:T(4,128)(2,1)}), bf16[64,4,192]{2,1,0:T(4,128)(2,1)S(1)}, u32[]{:S(2)}, u32[]{:S(2)}) %all-to-all-start.3) | async-done | bytes 98336 | tf_op jit(solution)/shard_map/all_to_all | solution.py:138
  287.5 0.7 copy.88
  288.2 1.0 dot_general.32
  289.2 1.5 fusion.28
  290.8 1.4 fusion.3
  292.2 5.2 %copy.90 = f32[144,64,128]{2,1,0:T(8,128)} copy(f32[144,64,128]{2,1,0:T(8,128)} %all-reduce.2.cloned.1.call-done) | data formatting | bytes 9437184
  (35 shorter events, 0.7 us)
Async XLA Ops:
  7.2 154.9 %copy-start = (bf16[144,64,128]{2,1,0:T(8,128)(2,1)S(1)}, bf16[144,64,128]{2,1,0:T(8,128)(2,1)}, u32[]{:S(2)}) copy-start(bf16[144,64,128]{2,1,0:T(8,128)(2,1)} %param.11) | copy-start | bytes 7077892
  11.9 1.6 copy-start.4
  11.9 1.9 copy-start.5
  12.0 2.9 copy-start.6
  13.5 1.4 copy-start.1
  13.5 1.4 copy-start.2
  13.5 1.6 copy-start.3
  15.1 11.1 %copy-start.11 = (s32[1,32]{1,0:T(1,128)S(1)}, s32[1,32]{1,0:T(1,128)}, u32[]{:S(2)}) copy-start(s32[1,32]{1,0:T(1,128)} %param.12) | copy-start | bytes 388
  18.4 17.5 %all-to-all-start = ((bf16[4,128,192]{2,0,1:T(4,128)(2,1)}), bf16[4,128,192]{2,0,1:T(4,128)(2,1)}, u32[]{:S(2)}, u32[]{:S(2)}) async-start(bf16[4,128,192]{2,0,1:T(4,128)(2,1)} %copy.52), calls=%async_computation | async-start | bytes 524288 | tf_op jit(solution)/shard_map/all_to_all | solution.py:116
  25.9 266.3 %all-reduce.2.cloned.1.call-start = ((), (), s32[]{:S(2)}) async-start(), calls=%async_computation.4 | async-start | bytes 9437184 | tf_op jit(solution)/shard_map/psum | solution.py:132
  26.6 15.2 %copy-start.8 = (bf16[96,64]{1,0:T(8,128)(2,1)}, bf16[96,64]{1,0:T(8,128)(2,1)S(1)}, u32[]{:S(2)}) copy-start(bf16[96,64]{1,0:T(8,128)(2,1)S(1)} %get-tuple-element.15) | copy-start | bytes 36868
  26.6 15.2 %copy-start.9 = (bf16[96,64]{1,0:T(8,128)(2,1)}, bf16[96,64]{1,0:T(8,128)(2,1)S(1)}, u32[]{:S(2)}) copy-start(bf16[96,64]{1,0:T(8,128)(2,1)S(1)} %get-tuple-element.16) | copy-start | bytes 36868
  167.1 48.3 %all-to-all-start.2 = ((bf16[64,2,2,2,144]{4,3,2,1,0:T(2,128)(2,1)}), bf16[64,2,2,2,144]{4,3,2,1,0:T(2,128)(2,1)}, u32[]{:S(2)}, u32[]{:S(2)}) async-start(bf16[64,2,2,2,144]{4,3,2,1,0:T(2,128)(2,1)} %bitcast.98), calls=%async_computation.2 | async-start | bytes 524288 | tf_op jit(solution)/shard_map/all_to_all | solution.py:133
  272.5 18.2 %copy-start.10 = (bf16[64,64]{1,0:T(8,128)(2,1)S(1)}, bf16[64,64]{1,0:T(8,128)(2,1)}, u32[]{:S(2)}) copy-start(bf16[64,64]{1,0:T(8,128)(2,1)} %param.10) | copy-start | bytes 24580
  274.2 13.2 %all-to-all-start.3 = ((bf16[64,4,192]{2,1,0:T(4,128)(2,1)}), bf16[64,4,192]{2,1,0:T(4,128)(2,1)S(1)}, u32[]{:S(2)}, u32[]{:S(2)}) async-start(bf16[64,4,192]{2,1,0:T(4,128)(2,1)} %reshape.125), calls=%async_computation.3 | async-start | bytes 262144 | tf_op jit(solution)/shard_map/all_to_all | solution.py:138
  289.2 1.6 copy-start.7
Sparse Core Ops, SparseCore 0:
  162.2 119.0 all-reduce.1
where the time goes:
time: 309 us; the launch traced here: 304 us
  local copies, waits for them, and re-layouts  152 us (49%)
  blocking collectives  57.2 us (19%)
  other arithmetic  31.5 us (10%)
  starting transfers between devices  17.2 us (6%)
  matrix products  16.2 us (5%)
  waiting for transfers between devices  15.9 us (5%)
  between operations  14.3 us (5%)
    psum x1, blocking collectives, shards(): grad_weight = lax.psum(local_weight, ('batch', 'rows'))  42.4 us
    unnamed x31, local copies, waits for them, and re-layouts  36.7 us
    transpose x2, local copies, waits for them, and re-layouts, from_blocks(): shaped.transpose(4, 2, 0, 1, 5, 3)  22.3 us
    concatenate x2, local copies, waits for them, and re-layouts, row_adjoint(): joined = jnp.concatenate([upper, lower], axis=0)  18.2 us
    all_to_all x1, blocking collectives, shards(): lax.all_to_all(to_blocks(spectra, PA), 'rows', split_axis=4, concat_axis=...  14.7 us
    another operation x2, local copies, waits for them, and re-layouts, row_combine(): jnp.stack([real_part, imag_part], axis=2) * scale  12.3 us
    all_to_all x1, local copies, waits for them, and re-layouts, shards(): lax.all_to_all(to_blocks(spectra, PA), 'rows', split_axis=4, concat_axis=...  12.1 us
    all_to_all x1, waiting for transfers between devices, shards(): lax.all_to_all(colspec, 'rows', split_axis=1, concat_axis=0, tiled=True)  9.32 us
  transfers between devices with their start and end apart: 4, of which 2 were waited for; matrix products, arithmetic and copies ran while one was open for 24% of the time, Pallas kernels for 0%

commit v1 on v0

--- a/solution.py
+++ b/solution.py
@@ -147,7 +147,7 @@
         "ric,roc->rio", masked_in, grad_pre, preferred_element_type=jnp.float32
     )
     local_weight = jnp.sum(row_partial, axis=0)
-    grad_weight = lax.psum(local_weight, ("batch", "rows"))
+    grad_weight = jax.lax.psum(jax.lax.psum(local_weight, "rows"), "batch")
     grad_weight = grad_weight * (1.0 / math.sqrt(batch_devices * active * SLAB * column_count))
     return (grad_input, grad_spectral, grad_weight)
 

time: 309 us -> 336 us (1.087)
  blocking collectives: 57.2 us -> 86.3 us
    psum x1 -> x2, blocking collectives: 42.4 us -> 71.6 us  [shards(): grad_weight = jax.lax.psum(jax.lax.psum(local_weight, 'rows'), 'batch')]
  transfers between devices with their start and end apart: 4 -> 4, of which waited for: 2 -> 2; matrix products, arithmetic and copies ran while one was open for 24% -> 22% of each run, Pallas kernels for 0% -> 0%
where the time goes in v1:
time: 336 us; the launch traced here: 331 us
  local copies, waits for them, and re-layouts  152 us (45%)
  blocking collectives  86.3 us (26%)
  other arithmetic  31.5 us (9%)
  matrix products  16.2 us (5%)
  waiting for transfers between devices  15.8 us (5%)
  starting transfers between devices  15.4 us (5%)
  between operations  14.3 us (4%)
    psum x2, blocking collectives, shards(): grad_weight = jax.lax.psum(jax.lax.psum(local_weight, 'rows'), 'batch')  71.6 us
    unnamed x31, local copies, waits for them, and re-layouts  36.7 us
    transpose x2, local copies, waits for them, and re-layouts, from_blocks(): shaped.transpose(4, 2, 0, 1, 5, 3)  22.3 us
    concatenate x2, local copies, waits for them, and re-layouts, row_adjoint(): joined = jnp.concatenate([upper, lower], axis=0)  18.2 us
    all_to_all x1, blocking collectives, shards(): lax.all_to_all(to_blocks(spectra, PA), 'rows', split_axis=4, concat_axis=...  14.7 us
    another operation x2, local copies, waits for them, and re-layouts, row_combine(): jnp.stack([real_part, imag_part], axis=2) * scale  12.3 us
    all_to_all x1, local copies, waits for them, and re-layouts, shards(): lax.all_to_all(to_blocks(spectra, PA), 'rows', split_axis=4, concat_axis=...  12.1 us
    all_to_all x1, waiting for transfers between devices, shards(): lax.all_to_all(colspec, 'rows', split_axis=1, concat_axis=0, tiled=True)  9.32 us
  transfers between devices with their start and end apart: 4, of which 2 were waited for; matrix products, arithmetic and copies ran while one was open for 22% of the time, Pallas kernels for 0%

profile of v1, /device:TPU:0, one launch (start us, length us, event | category | flops | bytes accessed | tf_op | source)
XLA Modules:
  0.0 331.4 jit_solution(9082142591100739380)
XLA Ops:
  7.2 3.9 %negate_convert_fusion = (bf16[2048,96]{0,1:T(8,128)(2,1)}, bf16[2048,96]{0,1:T(8,128)(2,1)}) fusion(), kind=kLoop, calls=%fused_computation.40 | loop fusion | flops 3342336 | bytes 786432 | tf_op jit(solution)/shard_map/convert.3
  11.0 0.7 dynamic-slice_bitcast_fusion
  12.0 1.4 bitcast_multiply_fusion
  13.5 0.3 copy-done.5
  13.8 1.1 fusion.15
  15.1 1.5 fusion.17
  16.6 1.8 copy.52
  18.4 7.5 %all-to-all-start = ((bf16[4,128,192]{2,0,1:T(4,128)(2,1)}), bf16[4,128,192]{2,0,1:T(4,128)(2,1)}, u32[]{:S(2)}, u32[]{:S(2)}) async-start(bf16[4,128,192]{2,0,1:T(4,128)(2,1)} %copy.52), calls=%async_computation | async-start | bytes 524288 | tf_op jit(solution)/shard_map/all_to_all | solution.py:116
  26.3 0.3 cosine_convert_fusion.1
  26.6 9.3 %all-to-all-done = bf16[4,128,192]{2,0,1:T(4,128)(2,1)} async-done(((bf16[4,128,192]{2,0,1:T(4,128)(2,1)}), bf16[4,128,192]{2,0,1:T(4,128)(2,1)}, u32[]{:S(2)}, u32[]{:S(2)}) %all-to-all-start) | async-done | bytes 196640 | tf_op jit(solution)/shard_map/all_to_all | solution.py:116
  35.9 1.0 copy.87
  36.9 0.7 copy.54
  37.6 1.9 reshape.119
  39.5 1.2 fusion.38
  40.7 1.1 fusion.43
  41.8 3.0 squeeze.7
  44.8 3.1 fusion.45
  47.9 4.2 %copy.79 = f32[96,8,1,96]{1,3,0,2:T(8,128)} copy(f32[96,8,1,96]{3,2,1,0:T(1,128)} %get-tuple-element.10) | data formatting | bytes 589824
  52.0 3.0 squeeze.8
  55.0 2.9 fusion.44
  58.0 4.2 %copy.80 = f32[96,8,1,96]{1,3,0,2:T(8,128)} copy(f32[96,8,1,96]{3,2,1,0:T(1,128)} %get-tuple-element.8) | data formatting | bytes 589824
  62.1 6.9 %sub.9 = f32[96,8,1,96]{1,3,0,2:T(8,128)} subtract(f32[96,8,1,96]{1,3,0,2:T(8,128)} %copy.79, f32[96,8,1,96]{1,3,0,2:T(8,128)} %copy.80) | non-fusion elementwise | flops 73728 | bytes 884736 | tf_op jit(solution)/shard_map/sub | solution.py:44
  69.1 6.2 %copy.60 = f32[48,2,8,1,48,2]{4,2,5,3,1,0:T(8,128)} copy(f32[48,2,8,1,48,2]{2,5,4,1,0,3:T(2,128)} %bitcast.84) | data formatting | bytes 589824 | tf_op jit(solution)/shard_map/stack | solution.py:45
  75.3 4.2 %copy.77 = f32[96,8,1,96]{1,3,0,2:T(8,128)} copy(f32[96,8,1,96]{3,2,1,0:T(1,128)} %get-tuple-element.9) | data formatting | bytes 589824
  79.4 4.2 %copy.78 = f32[96,8,1,96]{1,3,0,2:T(8,128)} copy(f32[96,8,1,96]{3,2,1,0:T(1,128)} %get-tuple-element.7) | data formatting | bytes 589824
  83.6 6.9 %add.62 = f32[96,8,1,96]{1,3,0,2:T(8,128)} add(f32[96,8,1,96]{1,3,0,2:T(8,128)} %copy.77, f32[96,8,1,96]{1,3,0,2:T(8,128)} %copy.78) | non-fusion elementwise | flops 73728 | bytes 884736 | tf_op jit(solution)/shard_map/add | solution.py:43
  90.5 6.2 %copy.59 = f32[48,2,8,1,48,2]{4,2,5,3,1,0:T(8,128)} copy(f32[48,2,8,1,48,2]{2,5,4,1,0,3:T(2,128)} %bitcast.85) | data formatting | bytes 589824 | tf_op jit(solution)/shard_map/stack | solution.py:45
  96.7 2.5 fusion.24
  99.2 9.3 %copy.74 = bf16[8,2,2,2,48,48]{0,3,2,1,5,4:T(2,128)(2,1)} copy(bf16[8,2,2,2,48,48]{5,0,3,1,2,4:T(8,128)(2,1)} %fusion.24) | data formatting | bytes 589824 | tf_op jit(solution)/shard_map/reshape | solution.py:51
  108.6 6.9 %reshape.131 = bf16[16,2,4608]{2,1,0:T(2,128)(2,1)} reshape(bf16[2304,2,2,2,8]{4,3,2,1,0:T(2,128)(2,1)} %bitcast.87) | data formatting | bytes 589824
  115.5 14.7 %all_to_all.60 = bf16[16,2,4608]{2,1,0:T(2,128)(2,1)} all-to-all(bf16[16,2,4608]{2,1,0:T(2,128)(2,1)} %reshape.131), channel_id=1, replica_groups=mesh['batch'=2,'rows'=16] {'rows'}, dimensions={0} | all-to-all | bytes 589824 | tf_op jit(solution)/shard_map/all_to_all | solution.py:124
  130.2 7.4 %reshape.132 = bf16[2304,2,2,2,8]{4,3,2,1,0:T(2,128)(2,1)} reshape(bf16[16,2,4608]{2,1,0:T(2,128)(2,1)} %all_to_all.60) | data formatting | bytes 589824
  137.6 12.1 %copy.75 = bf16[8,2,2,2,16,144]{5,4,0,3,2,1:T(8,128)(2,1)} copy(bf16[8,2,2,2,16,144]{0,3,2,1,5,4:T(2,128)(2,1)} %bitcast.88) | data formatting | bytes 589824 | tf_op jit(solution)/shard_map/all_to_all | solution.py:124
  149.7 1.8 fusion.46
  151.6 0.9 maximum_bitcast_fusion.1
  152.4 1.9 copy.65
  154.4 1.7 copy.85
  156.1 1.9 copy.73
  157.9 4.0 %fusion.48 = f32[144,64,128]{2,1,0:T(8,128)} fusion(bf16[144,64,8]{1,2,0:T(8,128)(2,1)} %bitcast.97, bf16[144,128,8]{1,2,0:T(8,128)(2,1)} %bitcast.91), kind=kOutput, calls=%fused_computation.85 | convolution fusion | flops 18874368 | bytes 5160960 | tf_op jit(solution)/shard_map/bik,bxk->bix/dot_general | solution.py:129
  162.0 3.0 convolution_convert_fusion
  165.0 2.0 copy.66
  167.0 4.2 %all-to-all-start.2 = ((bf16[64,2,2,2,144]{4,3,2,1,0:T(2,128)(2,1)}), bf16[64,2,2,2,144]{4,3,2,1,0:T(2,128)(2,1)}, u32[]{:S(2)}, u32[]{:S(2)}) async-start(bf16[64,2,2,2,144]{4,3,2,1,0:T(2,128)(2,1)} %bitcast.98), calls=%async_computation.2 | async-start | bytes 524288 | tf_op jit(solution)/shard_map/all_to_all | solution.py:133
  171.2 1.6 convolution_bitcast_fusion.1
  172.9 61.8 %psum.22 = f32[64,64]{1,0:T(8,128)S(1)} all-reduce(f32[64,64]{1,0:T(8,128)S(1)} %convolution_bitcast_fusion.1), channel_id=1, replica_groups=mesh['batch'=2,'rows'=16] {'rows'}, use_global_device_ids=true, to_apply=%region_1.2 | all-reduce | flops 4096 | bytes 32768 | tf_op jit(solution)/shard_map/psum | solution.py:150
  234.6 9.8 %psum.23 = f32[64,64]{1,0:T(8,128)} all-reduce(f32[64,64]{1,0:T(8,128)S(1)} %psum.22), channel_id=1, replica_groups=mesh['batch'=2,'rows'=16] {'batch'}, use_global_device_ids=true, to_apply=%region_2.3 | all-reduce | flops 4096 | bytes 32768 | tf_op jit(solution)/shard_map/psum | solution.py:150
  244.5 1.8 copy.67
  246.3 2.1 reshape.123
  248.4 13.8 %copy.69 = bf16[48,2,4,2,48,2]{2,5,4,3,1,0:T(2,128)(2,1)} copy(bf16[48,2,4,2,48,2]{4,0,5,1,3,2:T(8,128)(2,1)} %bitcast.89) | data formatting | bytes 294912 | tf_op jit(solution)/shard_map/transpose | solution.py:57
  262.3 8.4 %copy.68 = bf16[48,2,4,2,48,2]{5,4,3,2,1,0:T(8,128)(2,1)} copy(bf16[48,2,4,2,48,2]{4,0,5,1,3,2:T(8,128)(2,1)} %bitcast.90) | data formatting | bytes 294912 | tf_op jit(solution)/shard_map/transpose | solution.py:57
  270.7 2.9 slice_negate_fusion
  273.6 3.1 pad_maximum_fusion
  276.7 4.8 %copy.70 = bf16[96,4,2,96]{3,2,1,0:T(2,128)(2,1)} copy(bf16[96,4,2,96]{1,3,2,0:T(8,128)(2,1)} %pad_maximum_fusion) | data formatting | bytes 294912 | tf_op jit(solution)/shard_map/stack | solution.py:83
  281.5 1.1 concatenate.28
  282.6 17.1 %concatenate.27 = bf16[96,768]{1,0:T(8,128)(2,1)} reshape(bf16[48,2,4,2,48,2]{5,4,3,2,1,0:T(8,128)(2,1)} %copy.68) | data formatting | bytes 294912 | tf_op jit(solution)/shard_map/concatenate | solution.py:84
  299.7 1.8 fusion.20
  301.5 1.7 reshape.125
  303.2 3.5 %all-to-all-start.3 = ((bf16[64,4,192]{2,1,0:T(4,128)(2,1)}), bf16[64,4,192]{2,1,0:T(4,128)(2,1)S(1)}, u32[]{:S(2)}, u32[]{:S(2)}) async-start(bf16[64,4,192]{2,1,0:T(4,128)(2,1)} %reshape.125), calls=%async_computation.3 | async-start | bytes 262144 | tf_op jit(solution)/shard_map/all_to_all | solution.py:138
  306.7 1.4 broadcast_multiply_fusion
  308.1 6.5 %all-to-all-done.3 = bf16[64,4,192]{2,1,0:T(4,128)(2,1)S(1)} async-done(((bf16[64,4,192]{2,1,0:T(4,128)(2,1)}), bf16[64,4,192]{2,1,0:T(4,128)(2,1)S(1)}, u32[]{:S(2)}, u32[]{:S(2)}) %all-to-all-start.3) | async-done | bytes 98336 | tf_op jit(solution)/shard_map/all_to_all | solution.py:138
  314.6 0.7 copy.88
  315.3 1.0 dot_general.32
  316.3 1.5 fusion.28
  317.9 1.4 fusion.3
  319.3 5.2 %copy.90 = f32[144,64,128]{2,1,0:T(8,128)} copy(f32[144,64,128]{2,1,0:T(8,128)} %all-reduce.2.cloned.1.call-done) | data formatting | bytes 9437184
  (36 shorter events, 0.9 us)
Async XLA Ops:
  7.2 154.8 %copy-start = (bf16[144,64,128]{2,1,0:T(8,128)(2,1)S(1)}, bf16[144,64,128]{2,1,0:T(8,128)(2,1)}, u32[]{:S(2)}) copy-start(bf16[144,64,128]{2,1,0:T(8,128)(2,1)} %param.11) | copy-start | bytes 7077892
  11.9 1.6 copy-start.4
  11.9 1.9 copy-start.5
  12.0 2.9 copy-start.6
  13.5 1.4 copy-start.1
  13.5 1.4 copy-start.2
  13.5 1.6 copy-start.3
  15.0 11.0 %copy-start.11 = (s32[1,32]{1,0:T(1,128)S(1)}, s32[1,32]{1,0:T(1,128)}, u32[]{:S(2)}) copy-start(s32[1,32]{1,0:T(1,128)} %param.12) | copy-start | bytes 388
  18.4 17.5 %all-to-all-start = ((bf16[4,128,192]{2,0,1:T(4,128)(2,1)}), bf16[4,128,192]{2,0,1:T(4,128)(2,1)}, u32[]{:S(2)}, u32[]{:S(2)}) async-start(bf16[4,128,192]{2,0,1:T(4,128)(2,1)} %copy.52), calls=%async_computation | async-start | bytes 524288 | tf_op jit(solution)/shard_map/all_to_all | solution.py:116
  25.9 293.4 %all-reduce.2.cloned.1.call-start = ((), (), s32[]{:S(2)}) async-start(), calls=%async_computation.4 | async-start | bytes 9437184 | tf_op jit(solution)/shard_map/psum | solution.py:132
  26.6 15.2 %copy-start.8 = (bf16[96,64]{1,0:T(8,128)(2,1)}, bf16[96,64]{1,0:T(8,128)(2,1)S(1)}, u32[]{:S(2)}) copy-start(bf16[96,64]{1,0:T(8,128)(2,1)S(1)} %get-tuple-element.15) | copy-start | bytes 36868
  26.6 15.2 %copy-start.9 = (bf16[96,64]{1,0:T(8,128)(2,1)}, bf16[96,64]{1,0:T(8,128)(2,1)S(1)}, u32[]{:S(2)}) copy-start(bf16[96,64]{1,0:T(8,128)(2,1)S(1)} %get-tuple-element.16) | copy-start | bytes 36868
  167.0 77.5 %all-to-all-start.2 = ((bf16[64,2,2,2,144]{4,3,2,1,0:T(2,128)(2,1)}), bf16[64,2,2,2,144]{4,3,2,1,0:T(2,128)(2,1)}, u32[]{:S(2)}, u32[]{:S(2)}) async-start(bf16[64,2,2,2,144]{4,3,2,1,0:T(2,128)(2,1)} %bitcast.98), calls=%async_computation.2 | async-start | bytes 524288 | tf_op jit(solution)/shard_map/all_to_all | solution.py:133
  301.5 16.4 %copy-start.10 = (bf16[64,64]{1,0:T(8,128)(2,1)S(1)}, bf16[64,64]{1,0:T(8,128)(2,1)}, u32[]{:S(2)}) copy-start(bf16[64,64]{1,0:T(8,128)(2,1)} %param.10) | copy-start | bytes 24580
  303.2 11.4 %all-to-all-start.3 = ((bf16[64,4,192]{2,1,0:T(4,128)(2,1)}), bf16[64,4,192]{2,1,0:T(4,128)(2,1)S(1)}, u32[]{:S(2)}, u32[]{:S(2)}) async-start(bf16[64,4,192]{2,1,0:T(4,128)(2,1)} %reshape.125), calls=%async_computation.3 | async-start | bytes 262144 | tf_op jit(solution)/shard_map/all_to_all | solution.py:138
  316.3 1.6 copy-start.7
Sparse Core Ops, SparseCore 0:
  162.1 118.3 all-reduce.1
